TPU v7x, 32 devices: a whole 2x2x4 slice. The times are simulated.
32 devices in a mesh: mem: 16 (over z, y, core), tile: 2 (over x).
Axes of the slice: x: 2, y: 2, z: 4, core: 2. Of those that a mesh axis runs over, the one named last changes fastest.
Arguments:
- member_perturbations: float32 [3, 32, 16, 256], P(None, 'mem', None, 'tile'), may hold values from -3 to 3
- obs_index: int32 [16, 2, 256], P('mem', 'tile'), may hold values from 0 to 383
- obs_value: float32 [16, 2, 256], P('mem', 'tile'), may hold values from -4 to 4
- obs_var: float32 [16, 2, 256], P('mem', 'tile'), may hold values from 0.05 to 0.5
- loc_weight: float32 [16, 2, 256], P('mem', 'tile'), may hold values from 0.2 to 1
Outputs:
- forecast: float32 [3, 32, 16, 256], P(None, 'mem', None, 'tile')
All inputs are finite; a program needn't handle non-finite values.
Results may differ from a plain program's by a relative error of at most 0.0003.
Values sent between devices are 32-bit elements; how exact they have to be, the bound alone decides.
A program may use at most 64 MiB of HBM per device.

v0:
```python
import jax
import jax.numpy as jnp
from jax import lax
from jax.sharding import PartitionSpec as P

PCELL = 128
NSIT = 6
mean_depth = 4.0
gravity = 0.25
coriolis = 0.1
time_step = 0.3
highest = lax.Precision.HIGHEST


def with_halo(cells, sides, width):
    for axis, dim in sides:
        count = lax.axis_size(axis)
        head = lax.slice_in_dim(cells, 0, width, axis=dim)
        tail = lax.slice_in_dim(cells, cells.shape[dim] - width, cells.shape[dim], axis=dim)
        cells = jnp.concatenate(
            [
                lax.ppermute(tail, axis, [(i, (i + 1) % count) for i in range(count)]),
                cells,
                lax.ppermute(head, axis, [((i + 1) % count, i) for i in range(count)]),
            ],
            axis=dim,
        )
    return cells


def middle(field):
    return field[..., 1:-1]


def across(field):
    return (field[..., 2:] - field[..., :-2]) * 0.5


def along(field):
    inner = middle(field)
    return (jnp.roll(inner, -1, -2) - jnp.roll(inner, 1, -2)) * 0.5


def tendency(extended):
    height = extended[0]
    east_wind = extended[1]
    north_wind = extended[2]
    depth_total = mean_depth + height
    east_mid = middle(east_wind)
    north_mid = middle(north_wind)
    d_height = -(across(depth_total * east_wind) + along(depth_total * north_wind))
    d_east = (
        -(east_mid * across(east_wind) + north_mid * along(east_wind))
        - gravity * across(height)
        + coriolis * north_mid
    )
    d_north = (
        -(east_mid * across(north_wind) + north_mid * along(north_wind))
        - gravity * along(height)
        - coriolis * east_mid
    )
    return jnp.stack([d_height, d_east, d_north])


def lead_interval_number(dynamics_variables):
    extended = with_halo(dynamics_variables, (("tile", 3),), 4)
    first_slope = tendency(extended)
    slope_two = tendency(extended[..., 1:-1] + 0.5 * time_step * first_slope)
    slope_three = tendency(extended[..., 2:-2] + 0.5 * time_step * slope_two)
    slope_four = tendency(extended[..., 3:-3] + time_step * slope_three)
    dynamics_variables = dynamics_variables + time_step / 6.0 * (
        first_slope[..., 3:-3]
        + 2.0 * slope_two[..., 2:-2]
        + 2.0 * slope_three[..., 1:-1]
        + slope_four
    )
    return dynamics_variables


def product(left, right):
    return jnp.einsum("rbij,rbjk->rbik", left, right, precision=highest)


def analyse(blocks, indices, values, variances, locality):
    members = blocks.shape[1]
    row_count = blocks.shape[2]
    block_count = blocks.shape[3]
    cells = blocks.shape[4]
    xbar = jnp.mean(blocks, axis=1, keepdims=True)
    pert = blocks - xbar
    flat = jnp.transpose(blocks, (2, 3, 0, 4, 1)).reshape(
        row_count, block_count, 3 * cells, members
    )
    observed = jnp.take_along_axis(flat, indices[..., None], axis=2)
    ybar = jnp.mean(observed, axis=3, keepdims=True)
    obs_pert = observed - ybar
    weighted = obs_pert * (locality / variances)[..., None]
    gram = jnp.einsum("rboi,rboj->rbij", weighted, obs_pert, precision=highest)
    identity = jnp.eye(members, dtype=jnp.float32)
    amat = gram + (members - 1.0) * identity
    frob = jnp.sqrt(jnp.sum(amat * amat, axis=(2, 3), keepdims=True))
    ymat = amat / frob
    zmat = jnp.broadcast_to(identity, amat.shape)
    for _ in range(NSIT):
        newton = 1.5 * identity - 0.5 * product(zmat, ymat)
        ymat = product(ymat, newton)
        zmat = product(newton, zmat)
    prec = product(zmat, zmat) / frob
    wmat = jnp.sqrt((members - 1.0) / frob) * zmat
    innov = values - ybar[..., 0]
    projected = jnp.einsum("rbok,rbo->rbk", weighted, innov, precision=highest)
    wbar = jnp.einsum("rbij,rbj->rbi", prec, projected, precision=highest)
    wtot = wmat + wbar[..., None]
    return xbar + jnp.einsum("virbc,rbij->vjrbc", pert, wtot, precision=highest)


def local(member_perturbations, obs_index, obs_value, obs_var, loc_weight):
    background_member_set = lead_interval_number(member_perturbations)
    patches = lax.all_to_all(background_member_set, "mem", split_axis=2, concat_axis=1, tiled=True)
    members = patches.shape[1]
    row_count = patches.shape[2]
    columns = patches.shape[3]
    blocks = patches.reshape(3, members, row_count, columns // PCELL, PCELL)
    updated_member_set = analyse(blocks, obs_index, obs_value, obs_var, loc_weight)
    closing_solution = lax.all_to_all(
        updated_member_set.reshape(3, members, row_count, columns),
        "mem",
        split_axis=1,
        concat_axis=2,
        tiled=True,
    )
    return lead_interval_number(closing_solution)


def solution(mesh):
    in_specs = (
        P(None, "mem", None, "tile"),
        P("mem", "tile", None),
        P("mem", "tile", None),
        P("mem", "tile", None),
        P("mem", "tile", None),
    )
    out_specs = P(None, "mem", None, "tile")
    return jax.shard_map(local, mesh=mesh, in_specs=in_specs, out_specs=out_specs, check_vma=False)
```

profile of v0, /device:TPU:0, one launch (start us, length us, event | category | flops | bytes accessed | tf_op | source)
XLA Modules:
  0.0 52.4 jit_solution(7982997128042682452)
XLA Ops:
  0.0 1.0 %fusion.239 = (f32[3,2,16,4]{3,2,1,0:T(8,128)S(1)}, f32[3,2,16,4]{3,2,1,0:T(8,128)S(1)}) fusion(f32[3,2,16,128]{3,2,1,0:T(8,128)} %param.5), kind=kLoop, calls=%fused_computation.385 | loop fusion | bytes 6144 | tf_op jit(solution)/shard_map/slice | solution.py:19
  1.0 3.0 %collective-permute-start = (f32[3,2,16,4]{3,2,1,0:T(8,128)S(1)}, f32[3,2,16,4]{3,2,1,0:T(8,128)S(1)}, u32[]{:S(2)}, u32[]{:S(2)}) collective-permute-start(f32[3,2,16,4]{3,2,1,0:T(8,128)S(1)} %get-tuple-element.59), channel_id=1, source_target_pairs={{0,1},{1,0},{2,3},{3,2},{4,5},{5,4},{6,7},{7,6},{8,9},{9,8},{10,11... | collective-permute-start | bytes 4616 | tf_op jit(solution)/shard_map/ppermute | solution.py:22
  4.1 0.7 %copy-done.2 = f32[1,1,256]{2,1,0:T(1,128)S(1)} copy-done((f32[1,1,256]{2,1,0:T(1,128)S(1)}, f32[1,1,256]{2,1,0:T(1,128)}, u32[]{:S(2)}) %copy-start.2) | copy-done | bytes 1048
  4.8 1.3 %collective-permute-done = f32[3,2,16,4]{3,2,1,0:T(8,128)S(1)} collective-permute-done((f32[3,2,16,4]{3,2,1,0:T(8,128)S(1)}, f32[3,2,16,4]{3,2,1,0:T(8,128)S(1)}, u32[]{:S(2)}, u32[]{:S(2)}) %collective-permute-start) | collective-permute-done | bytes 1568 | tf_op jit(solution)/shard_map/ppermute | solution.py:22
  6.1 2.0 %collective-permute-done.1 = f32[3,2,16,4]{3,2,1,0:T(8,128)S(1)} collective-permute-done((f32[3,2,16,4]{3,2,1,0:T(8,128)S(1)}, f32[3,2,16,4]{3,2,1,0:T(8,128)S(1)}, u32[]{:S(2)}, u32[]{:S(2)}) %collective-permute-start.1) | collective-permute-done | bytes 1568 | tf_op jit(solution)/shard_map/ppermute | solution.py:24
  12.4 0.7 %copy.57 = f32[3,2,16,128]{3,0,1,2:T(4,128)} copy(f32[3,2,16,128]{3,2,1,0:T(8,128)S(1)} %fusion.33) | data formatting | bytes 98304 | tf_op jit(solution)/shard_map/add | solution.py:71
  13.0 5.9 %all-to-all-start = ((f32[3,2,16,128]{3,0,1,2:T(4,128)}), f32[3,2,16,128]{3,0,1,2:T(4,128)S(1)}, u32[]{:S(2)}, u32[]{:S(2)}) async-start(f32[3,2,16,128]{3,0,1,2:T(4,128)} %copy.57), calls=%async_computation | async-start | bytes 131072 | tf_op jit(solution)/shard_map/all_to_all | solution.py:119
  19.0 6.9 %all-to-all-done = f32[3,2,16,128]{3,0,1,2:T(4,128)S(1)} async-done(((f32[3,2,16,128]{3,0,1,2:T(4,128)}), f32[3,2,16,128]{3,0,1,2:T(4,128)S(1)}, u32[]{:S(2)}, u32[]{:S(2)}) %all-to-all-start) | async-done | bytes 49184 | tf_op jit(solution)/shard_map/all_to_all | solution.py:119
  26.0 0.7 %gather_fusion = f32[256,32]{1,0:T(8,128)S(1)} fusion(f32[384,32]{1,0:T(8,128)S(1)} %bitcast.274, s32[1024]{0:T(1024)S(1)} %pad_clamp_fusion), kind=kCustom, calls=%fused_computation | custom fusion | bytes 66560 | tf_op jit(solution)/shard_map/jit(take_along_axis)/gather | solution.py:94
  26.8 0.2 fusion.13
  26.9 1.2 %multiply_reduce_fusion = (f32[]{:T(128)}, f32[32,32]{1,0:T(8,128)S(1)}) fusion(f32[256,32]{1,0:T(8,128)S(1)} %gather_fusion, f32[256]{0:T(256)S(1)} %broadcast_multiply_fusion.1, pred[256]{0:T(512)(128)(4,1)S(1)} %compare_and_fusion, f32[256]{0:T(256)S(1)} %bitcast.283), kind=kOutput, calls=%fused_computation.366 | convolution fusion | flops 3191807 | bytes 39172 | tf_op jit(solution)/shard_map/rboi,rboj->rbij/dot_general | solution.py:98
  28.9 0.1 fusion.233
  29.2 0.2 fusion.6
  29.5 0.1 fusion.304
  29.7 0.2 fusion.5
  30.0 0.1 fusion.306
  30.1 0.2 fusion.4
  30.4 0.1 fusion.308
  30.6 0.2 fusion.3
  30.9 0.1 fusion.310
  31.1 0.2 fusion.2
  31.4 0.2 convolution_divide_fusion
  31.7 0.7 %copy-done.4 = f32[1,1,256]{2,1,0:T(1,128)S(1)} copy-done((f32[1,1,256]{2,1,0:T(1,128)S(1)}, f32[1,1,256]{2,1,0:T(1,128)}, u32[]{:S(2)}) %copy-start.4) | copy-done | bytes 1048
  32.4 0.3 convolution_bitcast_fusion.2
  32.7 0.1 convolution_bitcast_fusion.1
  32.9 0.3 fusion.1
  33.3 9.3 %all_to_all.33 = f32[3,32,1,128]{3,2,0,1:T(1,128)S(1)} all-to-all(f32[3,32,1,128]{3,2,0,1:T(1,128)S(1)} %copy.62), channel_id=1, replica_groups=mesh['mem'=16,'tile'=2] {'mem'}, dimensions={1} | all-to-all | bytes 98304 | tf_op jit(solution)/shard_map/all_to_all | solution.py:125
  42.7 0.5 %collective-permute-start.2 = (f32[3,2,16,4]{3,2,1,0:T(8,128)S(1)}, f32[3,2,16,4]{3,2,1,0:T(8,128)S(1)}, u32[]{:S(2)}, u32[]{:S(2)}) collective-permute-start(f32[3,2,16,4]{3,2,1,0:T(8,128)S(1)} %get-tuple-element.57), channel_id=1, source_target_pairs={{0,1},{1,0},{2,3},{3,2},{4,5},{5,4},{6,7},{7,6},{8,9},{9,8},{10,11... | collective-permute-start | bytes 4616 | tf_op jit(solution)/shard_map/ppermute | solution.py:22
  43.3 1.5 %collective-permute-start.3 = (f32[3,2,16,4]{3,2,1,0:T(8,128)S(1)}, f32[3,2,16,4]{3,2,1,0:T(8,128)S(1)}, u32[]{:S(2)}, u32[]{:S(2)}) collective-permute-start(f32[3,2,16,4]{3,2,1,0:T(8,128)S(1)} %get-tuple-element.58), channel_id=1, source_target_pairs={{1,0},{0,1},{3,2},{2,3},{5,4},{4,5},{7,6},{6,7},{9,8},{8,9},{11,10... | collective-permute-start | bytes 4616 | tf_op jit(solution)/shard_map/ppermute | solution.py:24
  44.7 2.1 %collective-permute-done.2 = f32[3,2,16,4]{3,2,1,0:T(8,128)S(1)} collective-permute-done((f32[3,2,16,4]{3,2,1,0:T(8,128)S(1)}, f32[3,2,16,4]{3,2,1,0:T(8,128)S(1)}, u32[]{:S(2)}, u32[]{:S(2)}) %collective-permute-start.2) | collective-permute-done | bytes 1568 | tf_op jit(solution)/shard_map/ppermute | solution.py:22
  46.8 0.5 %collective-permute-done.3 = f32[3,2,16,4]{3,2,1,0:T(8,128)S(1)} collective-permute-done((f32[3,2,16,4]{3,2,1,0:T(8,128)S(1)}, f32[3,2,16,4]{3,2,1,0:T(8,128)S(1)}, u32[]{:S(2)}, u32[]{:S(2)}) %collective-permute-start.3) | collective-permute-done | bytes 1568 | tf_op jit(solution)/shard_map/ppermute | solution.py:24
  51.6 0.7 %fusion.28 = f32[3,2,16,128]{3,2,1,0:T(8,128)} fusion(f32[3,2,16,130]{3,2,1,0:T(8,128)S(1)} %get-tuple-element.11, f32[3,2,16,132]{3,2,1,0:T(8,128)S(1)} %get-tuple-element.14, f32[3,2,16,134]{3,2,1,0:T(8,128)S(1)} %get-tuple-element.12, f32[1,2,16,128]{3,2,1,0:T(8,128)S(1)} %fusion.185, f32[1,2,16,128]{3,2,1,0:T(8,128)S(1)} %fusion.189, ...), kind=kLoop, calls=%fused_computation.55 | loop fusion | flops 110592 | bytes 294912 | tf_op jit(solution)/shard_map/add | solution.py:71
  (142 shorter events, 9.7 us)
Async XLA Ops:
  0.0 8.1 %copy-start = (f32[3,2,16,128]{3,2,1,0:T(8,128)S(1)}, f32[3,2,16,128]{3,2,1,0:T(8,128)}, u32[]{:S(2)}) copy-start(f32[3,2,16,128]{3,2,1,0:T(8,128)} %param.5) | copy-start | bytes 147460
  1.0 3.1 %copy-start.3 = (s32[1,1,256]{2,1,0:T(1,128)S(1)}, s32[1,1,256]{2,1,0:T(1,128)}, u32[]{:S(2)}) copy-start(s32[1,1,256]{2,1,0:T(1,128)} %param.6) | copy-start | bytes 3076
  1.0 5.1 %collective-permute-start = (f32[3,2,16,4]{3,2,1,0:T(8,128)S(1)}, f32[3,2,16,4]{3,2,1,0:T(8,128)S(1)}, u32[]{:S(2)}, u32[]{:S(2)}) collective-permute-start(f32[3,2,16,4]{3,2,1,0:T(8,128)S(1)} %get-tuple-element.59), channel_id=1, source_target_pairs={{0,1},{1,0},{2,3},{3,2},{4,5},{5,4},{6,7},{7,6},{8,9},{9,8},{10,11... | collective-permute-start | bytes 4616 | tf_op jit(solution)/shard_map/ppermute | solution.py:22
  4.0 4.1 %collective-permute-start.1 = (f32[3,2,16,4]{3,2,1,0:T(8,128)S(1)}, f32[3,2,16,4]{3,2,1,0:T(8,128)S(1)}, u32[]{:S(2)}, u32[]{:S(2)}) collective-permute-start(f32[3,2,16,4]{3,2,1,0:T(8,128)S(1)} %get-tuple-element.60), channel_id=1, source_target_pairs={{1,0},{0,1},{3,2},{2,3},{5,4},{4,5},{7,6},{6,7},{9,8},{8,9},{11,10... | collective-permute-start | bytes 4616 | tf_op jit(solution)/shard_map/ppermute | solution.py:24
  4.1 0.7 %copy-start.2 = (f32[1,1,256]{2,1,0:T(1,128)S(1)}, f32[1,1,256]{2,1,0:T(1,128)}, u32[]{:S(2)}) copy-start(f32[1,1,256]{2,1,0:T(1,128)} %param.8) | copy-start | bytes 3076
  4.1 0.7 %copy-start.1 = (f32[1,1,256]{2,1,0:T(1,128)S(1)}, f32[1,1,256]{2,1,0:T(1,128)}, u32[]{:S(2)}) copy-start(f32[1,1,256]{2,1,0:T(1,128)} %param.9) | copy-start | bytes 3076
  13.0 12.8 %all-to-all-start = ((f32[3,2,16,128]{3,0,1,2:T(4,128)}), f32[3,2,16,128]{3,0,1,2:T(4,128)S(1)}, u32[]{:S(2)}, u32[]{:S(2)}) async-start(f32[3,2,16,128]{3,0,1,2:T(4,128)} %copy.57), calls=%async_computation | async-start | bytes 131072 | tf_op jit(solution)/shard_map/all_to_all | solution.py:119
  31.7 0.7 %copy-start.4 = (f32[1,1,256]{2,1,0:T(1,128)S(1)}, f32[1,1,256]{2,1,0:T(1,128)}, u32[]{:S(2)}) copy-start(f32[1,1,256]{2,1,0:T(1,128)} %param.7) | copy-start | bytes 3076
  42.7 4.1 %collective-permute-start.2 = (f32[3,2,16,4]{3,2,1,0:T(8,128)S(1)}, f32[3,2,16,4]{3,2,1,0:T(8,128)S(1)}, u32[]{:S(2)}, u32[]{:S(2)}) collective-permute-start(f32[3,2,16,4]{3,2,1,0:T(8,128)S(1)} %get-tuple-element.57), channel_id=1, source_target_pairs={{0,1},{1,0},{2,3},{3,2},{4,5},{5,4},{6,7},{7,6},{8,9},{9,8},{10,11... | collective-permute-start | bytes 4616 | tf_op jit(solution)/shard_map/ppermute | solution.py:22
  43.3 4.1 %collective-permute-start.3 = (f32[3,2,16,4]{3,2,1,0:T(8,128)S(1)}, f32[3,2,16,4]{3,2,1,0:T(8,128)S(1)}, u32[]{:S(2)}, u32[]{:S(2)}) collective-permute-start(f32[3,2,16,4]{3,2,1,0:T(8,128)S(1)} %get-tuple-element.58), channel_id=1, source_target_pairs={{1,0},{0,1},{3,2},{2,3},{5,4},{4,5},{7,6},{6,7},{9,8},{8,9},{11,10... | collective-permute-start | bytes 4616 | tf_op jit(solution)/shard_map/ppermute | solution.py:24
where the time goes:
time: 52.7 us; the launch traced here: 52.4 us
  waiting for transfers between devices  12.8 us (24%)
  starting transfers between devices  11.1 us (21%)
  blocking collectives  9.34 us (18%)
  local copies, waits for them, and re-layouts  9.04 us (17%)
  matrix products  4.63 us (9%)
  other arithmetic  4.22 us (8%)
  between operations  1.26 us (2%)
    all_to_all x1, blocking collectives, local(): lax.all_to_all(updated_member_set.reshape(3, members, row_count, columns)...  9.34 us
    all_to_all x1, waiting for transfers between devices, local(): lax.all_to_all(background_member_set, 'mem', split_axis=2, concat_axis=1,...  6.88 us
    all_to_all x1, starting transfers between devices, local(): lax.all_to_all(background_member_set, 'mem', split_axis=2, concat_axis=1,...  5.94 us
    slice x62, local copies, waits for them, and re-layouts, along(): return (jnp.roll(inner, -1, -2) - jnp.roll(inner, 1, -2)) * 0.5  4.91 us
    ppermute x2, starting transfers between devices, with_halo(): lax.ppermute(tail, axis, [(i, (i + 1) % count) for i in range(count)])  3.57 us
    ppermute x2, waiting for transfers between devices, with_halo(): lax.ppermute(tail, axis, [(i, (i + 1) % count) for i in range(count)])  3.35 us
    dot_general x18, matrix products, product(): return jnp.einsum('rbij,rbjk->rbik', left, right, precision=highest)  2.66 us
    another operation x28, other arithmetic, tendency(): return jnp.stack([d_height, d_east, d_north])  2.64 us
  transfers between devices with their start and end apart: 5, of which 5 were waited for; matrix products, arithmetic and copies ran while one was open for 0% of the time, Pallas kernels for 0%

commit v1 on v0

--- a/solution.py
+++ b/solution.py
@@ -122,13 +122,11 @@
     columns = patches.shape[3]
     blocks = patches.reshape(3, members, row_count, columns // PCELL, PCELL)
     updated_member_set = analyse(blocks, obs_index, obs_value, obs_var, loc_weight)
-    closing_solution = lax.all_to_all(
-        updated_member_set.reshape(3, members, row_count, columns),
-        "mem",
-        split_axis=1,
-        concat_axis=2,
-        tiled=True,
-    )
+    part = updated_member_set.reshape(3, members, row_count, columns)
+    size = lax.axis_size("mem")
+    pieces = jnp.stack(jnp.split(part, size, axis=1), axis=0)
+    pieces = lax.all_to_all(pieces, "mem", split_axis=0, concat_axis=0)
+    closing_solution = jnp.concatenate(pieces, axis=2)
     return lead_interval_number(closing_solution)
 
 

time: 52.7 us -> 52.7 us (level)
    unnamed x10 -> x25, local copies, waits for them, and re-layouts: 1.35 us -> 1.51 us
where the time goes in v1:
time: 52.7 us; the launch traced here: 52.4 us
  waiting for transfers between devices  12.7 us (24%)
  starting transfers between devices  11.1 us (21%)
  blocking collectives  9.34 us (18%)
  local copies, waits for them, and re-layouts  9.13 us (17%)
  matrix products  4.63 us (9%)
  other arithmetic  4.22 us (8%)
  between operations  1.32 us (3%)
    all_to_all x1, blocking collectives, local(): pieces = lax.all_to_all(pieces, 'mem', split_axis=0, concat_axis=0)  9.34 us
    all_to_all x1, waiting for transfers between devices, local(): lax.all_to_all(background_member_set, 'mem', split_axis=2, concat_axis=1,...  6.75 us
    all_to_all x1, starting transfers between devices, local(): lax.all_to_all(background_member_set, 'mem', split_axis=2, concat_axis=1,...  5.94 us
    slice x62, local copies, waits for them, and re-layouts, along(): return (jnp.roll(inner, -1, -2) - jnp.roll(inner, 1, -2)) * 0.5  4.91 us
    ppermute x2, starting transfers between devices, with_halo(): lax.ppermute(tail, axis, [(i, (i + 1) % count) for i in range(count)])  3.57 us
    ppermute x2, waiting for transfers between devices, with_halo(): lax.ppermute(tail, axis, [(i, (i + 1) % count) for i in range(count)])  3.35 us
    dot_general x18, matrix products, product(): return jnp.einsum('rbij,rbjk->rbik', left, right, precision=highest)  2.66 us
    another operation x28, other arithmetic, tendency(): return jnp.stack([d_height, d_east, d_north])  2.64 us
  transfers between devices with their start and end apart: 5, of which 5 were waited for; matrix products, arithmetic and copies ran while one was open for 0% of the time, Pallas kernels for 0%

profile of v1, /device:TPU:0, one launch (start us, length us, event | category | flops | bytes accessed | tf_op | source)
XLA Modules:
  0.0 52.4 jit_solution(4519805021748958337)
XLA Ops:
  0.0 1.0 %fusion.239 = (f32[3,2,16,4]{3,2,1,0:T(8,128)S(1)}, f32[3,2,16,4]{3,2,1,0:T(8,128)S(1)}) fusion(f32[3,2,16,128]{3,2,1,0:T(8,128)} %param.5), kind=kLoop, calls=%fused_computation.417 | loop fusion | bytes 6144 | tf_op jit(solution)/shard_map/slice | solution.py:19
  1.0 3.0 %collective-permute-start = (f32[3,2,16,4]{3,2,1,0:T(8,128)S(1)}, f32[3,2,16,4]{3,2,1,0:T(8,128)S(1)}, u32[]{:S(2)}, u32[]{:S(2)}) collective-permute-start(f32[3,2,16,4]{3,2,1,0:T(8,128)S(1)} %get-tuple-element.59), channel_id=1, source_target_pairs={{0,1},{1,0},{2,3},{3,2},{4,5},{5,4},{6,7},{7,6},{8,9},{9,8},{10,11... | collective-permute-start | bytes 4616 | tf_op jit(solution)/shard_map/ppermute | solution.py:22
  4.1 0.7 %copy-done.2 = f32[1,1,256]{2,1,0:T(1,128)S(1)} copy-done((f32[1,1,256]{2,1,0:T(1,128)S(1)}, f32[1,1,256]{2,1,0:T(1,128)}, u32[]{:S(2)}) %copy-start.2) | copy-done | bytes 1048
  4.8 1.3 %collective-permute-done = f32[3,2,16,4]{3,2,1,0:T(8,128)S(1)} collective-permute-done((f32[3,2,16,4]{3,2,1,0:T(8,128)S(1)}, f32[3,2,16,4]{3,2,1,0:T(8,128)S(1)}, u32[]{:S(2)}, u32[]{:S(2)}) %collective-permute-start) | collective-permute-done | bytes 1568 | tf_op jit(solution)/shard_map/ppermute | solution.py:22
  6.1 2.0 %collective-permute-done.1 = f32[3,2,16,4]{3,2,1,0:T(8,128)S(1)} collective-permute-done((f32[3,2,16,4]{3,2,1,0:T(8,128)S(1)}, f32[3,2,16,4]{3,2,1,0:T(8,128)S(1)}, u32[]{:S(2)}, u32[]{:S(2)}) %collective-permute-start.1) | collective-permute-done | bytes 1568 | tf_op jit(solution)/shard_map/ppermute | solution.py:24
  12.4 0.6 %copy.54 = f32[3,2,16,128]{3,1,0,2:T(2,128)} copy(f32[3,2,16,128]{3,2,1,0:T(8,128)S(1)} %fusion.33) | data formatting | bytes 98304 | tf_op jit(solution)/shard_map/add | solution.py:71
  13.0 5.9 %all-to-all-start = ((f32[3,2,16,128]{3,1,0,2:T(2,128)}), f32[3,2,16,128]{3,1,0,2:T(2,128)S(1)}, u32[]{:S(2)}, u32[]{:S(2)}) async-start(f32[3,2,16,128]{3,1,0,2:T(2,128)} %copy.54), calls=%async_computation | async-start | bytes 98304 | tf_op jit(solution)/shard_map/all_to_all | solution.py:119
  19.0 6.8 %all-to-all-done = f32[3,2,16,128]{3,1,0,2:T(2,128)S(1)} async-done(((f32[3,2,16,128]{3,1,0,2:T(2,128)}), f32[3,2,16,128]{3,1,0,2:T(2,128)S(1)}, u32[]{:S(2)}, u32[]{:S(2)}) %all-to-all-start) | async-done | bytes 49184 | tf_op jit(solution)/shard_map/all_to_all | solution.py:119
  25.9 0.7 %gather_fusion = f32[256,32]{1,0:T(8,128)S(1)} fusion(f32[384,32]{1,0:T(8,128)S(1)} %bitcast.337, s32[1024]{0:T(1024)S(1)} %pad_clamp_fusion), kind=kCustom, calls=%fused_computation | custom fusion | bytes 66560 | tf_op jit(solution)/shard_map/jit(take_along_axis)/gather | solution.py:94
  26.6 0.2 fusion.13
  26.8 1.2 %multiply_reduce_fusion = (f32[]{:T(128)}, f32[32,32]{1,0:T(8,128)S(1)}) fusion(f32[256,32]{1,0:T(8,128)S(1)} %gather_fusion, f32[256]{0:T(256)S(1)} %broadcast_multiply_fusion.1, pred[256]{0:T(512)(128)(4,1)S(1)} %compare_and_fusion, f32[256]{0:T(256)S(1)} %bitcast.344), kind=kOutput, calls=%fused_computation.382 | convolution fusion | flops 3191807 | bytes 39172 | tf_op jit(solution)/shard_map/rboi,rboj->rbij/dot_general | solution.py:98
  28.8 0.1 fusion.233
  29.1 0.2 fusion.6
  29.4 0.1 fusion.304
  29.5 0.2 fusion.5
  29.8 0.1 fusion.306
  30.0 0.2 fusion.4
  30.3 0.1 fusion.308
  30.4 0.2 fusion.3
  30.8 0.1 fusion.310
  30.9 0.2 fusion.2
  31.2 0.2 convolution_divide_fusion
  31.6 0.7 %copy-done.4 = f32[1,1,256]{2,1,0:T(1,128)S(1)} copy-done((f32[1,1,256]{2,1,0:T(1,128)S(1)}, f32[1,1,256]{2,1,0:T(1,128)}, u32[]{:S(2)}) %copy-start.4) | copy-done | bytes 1048
  32.3 0.3 convolution_bitcast_fusion.2
  32.6 0.1 convolution_bitcast_fusion.1
  32.7 0.3 fusion.1
  33.3 9.3 %all_to_all.20 = f32[16,3,2,1,128]{4,2,1,3,0:T(2,128)S(1)} all-to-all(f32[16,3,2,1,128]{4,2,1,3,0:T(2,128)S(1)} %constant_dynamic-update-slice_fusion), channel_id=1, replica_groups=mesh['mem'=16,'tile'=2] {'mem'}, dimensions={0} | all-to-all | bytes 98304 | tf_op jit(solution)/shard_map/all_to_all | solution.py:128
  42.7 0.5 %collective-permute-start.2 = (f32[3,2,16,4]{3,2,1,0:T(8,128)S(1)}, f32[3,2,16,4]{3,2,1,0:T(8,128)S(1)}, u32[]{:S(2)}, u32[]{:S(2)}) collective-permute-start(f32[3,2,16,4]{3,2,1,0:T(8,128)S(1)} %get-tuple-element.57), channel_id=1, source_target_pairs={{0,1},{1,0},{2,3},{3,2},{4,5},{5,4},{6,7},{7,6},{8,9},{9,8},{10,11... | collective-permute-start | bytes 4616 | tf_op jit(solution)/shard_map/ppermute | solution.py:22
  43.3 1.5 %collective-permute-start.3 = (f32[3,2,16,4]{3,2,1,0:T(8,128)S(1)}, f32[3,2,16,4]{3,2,1,0:T(8,128)S(1)}, u32[]{:S(2)}, u32[]{:S(2)}) collective-permute-start(f32[3,2,16,4]{3,2,1,0:T(8,128)S(1)} %get-tuple-element.58), channel_id=1, source_target_pairs={{1,0},{0,1},{3,2},{2,3},{5,4},{4,5},{7,6},{6,7},{9,8},{8,9},{11,10... | collective-permute-start | bytes 4616 | tf_op jit(solution)/shard_map/ppermute | solution.py:24
  44.8 2.1 %collective-permute-done.2 = f32[3,2,16,4]{3,2,1,0:T(8,128)S(1)} collective-permute-done((f32[3,2,16,4]{3,2,1,0:T(8,128)S(1)}, f32[3,2,16,4]{3,2,1,0:T(8,128)S(1)}, u32[]{:S(2)}, u32[]{:S(2)}) %collective-permute-start.2) | collective-permute-done | bytes 1568 | tf_op jit(solution)/shard_map/ppermute | solution.py:22
  46.8 0.5 %collective-permute-done.3 = f32[3,2,16,4]{3,2,1,0:T(8,128)S(1)} collective-permute-done((f32[3,2,16,4]{3,2,1,0:T(8,128)S(1)}, f32[3,2,16,4]{3,2,1,0:T(8,128)S(1)}, u32[]{:S(2)}, u32[]{:S(2)}) %collective-permute-start.3) | collective-permute-done | bytes 1568 | tf_op jit(solution)/shard_map/ppermute | solution.py:24
  51.6 0.7 %fusion.28 = f32[3,2,16,128]{3,2,1,0:T(8,128)} fusion(f32[3,2,16,130]{3,2,1,0:T(8,128)S(1)} %get-tuple-element.11, f32[3,2,16,132]{3,2,1,0:T(8,128)S(1)} %get-tuple-element.14, f32[3,2,16,134]{3,2,1,0:T(8,128)S(1)} %get-tuple-element.12, f32[1,2,16,128]{3,2,1,0:T(8,128)S(1)} %fusion.185, f32[1,2,16,128]{3,2,1,0:T(8,128)S(1)} %fusion.189, ...), kind=kLoop, calls=%fused_computation.55 | loop fusion | flops 110592 | bytes 294912 | tf_op jit(solution)/shard_map/add | solution.py:71
  (156 shorter events, 9.8 us)
Async XLA Ops:
  0.0 8.1 %copy-start = (f32[3,2,16,128]{3,2,1,0:T(8,128)S(1)}, f32[3,2,16,128]{3,2,1,0:T(8,128)}, u32[]{:S(2)}) copy-start(f32[3,2,16,128]{3,2,1,0:T(8,128)} %param.5) | copy-start | bytes 147460
  1.0 3.1 %copy-start.3 = (s32[1,1,256]{2,1,0:T(1,128)S(1)}, s32[1,1,256]{2,1,0:T(1,128)}, u32[]{:S(2)}) copy-start(s32[1,1,256]{2,1,0:T(1,128)} %param.6) | copy-start | bytes 3076
  1.0 5.1 %collective-permute-start = (f32[3,2,16,4]{3,2,1,0:T(8,128)S(1)}, f32[3,2,16,4]{3,2,1,0:T(8,128)S(1)}, u32[]{:S(2)}, u32[]{:S(2)}) collective-permute-start(f32[3,2,16,4]{3,2,1,0:T(8,128)S(1)} %get-tuple-element.59), channel_id=1, source_target_pairs={{0,1},{1,0},{2,3},{3,2},{4,5},{5,4},{6,7},{7,6},{8,9},{9,8},{10,11... | collective-permute-start | bytes 4616 | tf_op jit(solution)/shard_map/ppermute | solution.py:22
  4.0 4.1 %collective-permute-start.1 = (f32[3,2,16,4]{3,2,1,0:T(8,128)S(1)}, f32[3,2,16,4]{3,2,1,0:T(8,128)S(1)}, u32[]{:S(2)}, u32[]{:S(2)}) collective-permute-start(f32[3,2,16,4]{3,2,1,0:T(8,128)S(1)} %get-tuple-element.60), channel_id=1, source_target_pairs={{1,0},{0,1},{3,2},{2,3},{5,4},{4,5},{7,6},{6,7},{9,8},{8,9},{11,10... | collective-permute-start | bytes 4616 | tf_op jit(solution)/shard_map/ppermute | solution.py:24
  4.1 0.7 %copy-start.2 = (f32[1,1,256]{2,1,0:T(1,128)S(1)}, f32[1,1,256]{2,1,0:T(1,128)}, u32[]{:S(2)}) copy-start(f32[1,1,256]{2,1,0:T(1,128)} %param.8) | copy-start | bytes 3076
  4.1 0.7 %copy-start.1 = (f32[1,1,256]{2,1,0:T(1,128)S(1)}, f32[1,1,256]{2,1,0:T(1,128)}, u32[]{:S(2)}) copy-start(f32[1,1,256]{2,1,0:T(1,128)} %param.9) | copy-start | bytes 3076
  13.0 12.7 %all-to-all-start = ((f32[3,2,16,128]{3,1,0,2:T(2,128)}), f32[3,2,16,128]{3,1,0,2:T(2,128)S(1)}, u32[]{:S(2)}, u32[]{:S(2)}) async-start(f32[3,2,16,128]{3,1,0,2:T(2,128)} %copy.54), calls=%async_computation | async-start | bytes 98304 | tf_op jit(solution)/shard_map/all_to_all | solution.py:119
  31.6 0.7 %copy-start.4 = (f32[1,1,256]{2,1,0:T(1,128)S(1)}, f32[1,1,256]{2,1,0:T(1,128)}, u32[]{:S(2)}) copy-start(f32[1,1,256]{2,1,0:T(1,128)} %param.7) | copy-start | bytes 3076
  42.7 4.1 %collective-permute-start.2 = (f32[3,2,16,4]{3,2,1,0:T(8,128)S(1)}, f32[3,2,16,4]{3,2,1,0:T(8,128)S(1)}, u32[]{:S(2)}, u32[]{:S(2)}) collective-permute-start(f32[3,2,16,4]{3,2,1,0:T(8,128)S(1)} %get-tuple-element.57), channel_id=1, source_target_pairs={{0,1},{1,0},{2,3},{3,2},{4,5},{5,4},{6,7},{7,6},{8,9},{9,8},{10,11... | collective-permute-start | bytes 4616 | tf_op jit(solution)/shard_map/ppermute | solution.py:22
  43.3 4.1 %collective-permute-start.3 = (f32[3,2,16,4]{3,2,1,0:T(8,128)S(1)}, f32[3,2,16,4]{3,2,1,0:T(8,128)S(1)}, u32[]{:S(2)}, u32[]{:S(2)}) collective-permute-start(f32[3,2,16,4]{3,2,1,0:T(8,128)S(1)} %get-tuple-element.58), channel_id=1, source_target_pairs={{1,0},{0,1},{3,2},{2,3},{5,4},{4,5},{7,6},{6,7},{9,8},{8,9},{11,10... | collective-permute-start | bytes 4616 | tf_op jit(solution)/shard_map/ppermute | solution.py:24
